TPU v7x, 512 devices: a whole 4x8x8 slice. The times are simulated.
512 devices in a mesh: state: 64 (over y_hi, z, x), lat: 8 (over y_lo, core).
Axes of the slice: x: 4, y: 8 (y_hi: 2, y_lo: 4; y = y_hi * 4 + y_lo), z: 8, core: 2. Of those that a mesh axis runs over, the one named last changes fastest.
Arguments:
- spins: int32 [64, 8, 128], P('state', 'lat'), may hold values from -1 to 1, as said below
- embed_w: bfloat16 [64, 9], replicated, may hold values from -2 to 2
- block_w: bfloat16 [16, 1, 2, 64, 576], replicated, may hold values from -0.25 to 0.25
- readout: bfloat16 [16, 64], replicated, may hold values from -0.09375 to 0.09375
- amp_cot: float32 [16, 64], replicated, may hold values from -6 to 6
Outputs:
- log_amp: float32 [16, 64], replicated
- block_grad: float32 [1024, 1, 2, 576], P('state')
- embed_grad: float32 [64, 9], replicated
Inputs may be any that keep to these rules, and one draw needn't show every extreme that they name: `spins`: every entry is -1 or +1.
All inputs are finite; a program needn't handle non-finite values.
Results may differ from a plain program's by a relative error of at most 0.00083.
Values may be sent and summed in bfloat16 or wider, within the bound.
No kernel may reach another device: no remote copies, remote signals or barrier semaphores. Data moves between devices by JAX's collectives and lax.ppermute only.
A program may use at most 64 MiB of HBM per device.

v0:
```python
import math
import jax
import jax.numpy as jnp
from jax import lax
from jax.sharding import PartitionSpec as P


def extended(block, sides, width):
    for axis, dim in sides:
        count = lax.axis_size(axis)
        forward = [(i, i + 1) for i in range(count - 1)]
        forward.append((count - 1, 0))
        backward = [(target, source) for source, target in forward]
        low = lax.ppermute(
            lax.slice_in_dim(block, block.shape[dim] - width, None, axis=dim), axis, forward
        )
        high = lax.ppermute(lax.slice_in_dim(block, 0, width, axis=dim), axis, backward)
        block = jnp.concatenate([low, block, high], axis=dim)
    return block


def swapped(value, axis, bit):
    mask = 2**bit
    pairs = [(source, source ^ mask) for source in range(lax.axis_size(axis))]
    return lax.ppermute(value, axis, pairs)


def make_patches(padded):
    row_count = padded.shape[2] - 2
    col_count = padded.shape[3] - 2
    pieces = []
    for step_x in range(3):
        for step_y in range(3):
            pieces.append(padded[:, :, step_x : step_x + row_count, step_y : step_y + col_count])
    return jnp.concatenate(pieces, axis=1)


def conv_apply(weight, patches):
    return jnp.einsum("ok,nkxy->noxy", weight, patches, preferred_element_type=jnp.float32)


def flipped(weight):
    out_count = weight.shape[0]
    in_count = weight.shape[1] // 9
    return jnp.transpose(weight.reshape(out_count, 9, in_count)[:, ::-1, :], (2, 1, 0)).reshape(
        in_count, 9 * out_count
    )


def grad_from(inner_field, cot_patches):
    channel_count = inner_field.shape[1]
    joined = jnp.einsum(
        "nqxy,nkxy->kq", inner_field, cot_patches, preferred_element_type=jnp.float32
    )
    turned = joined.reshape(9, -1, channel_count)[::-1]
    return jnp.transpose(turned, (1, 0, 2)).reshape(turned.shape[1], 9 * channel_count)


def spin_contract(cotan, padded):
    row_count = cotan.shape[2]
    col_count = cotan.shape[3]
    offset_parts = []
    for step_x in range(3):
        for step_y in range(3):
            window = padded[:, 0, step_x : step_x + row_count, step_y : step_y + col_count].astype(
                jnp.float32
            )
            offset_parts.append(
                jnp.einsum("ncxy,nxy->c", cotan, window, precision=lax.Precision.HIGHEST)
            )
    return jnp.stack(offset_parts, axis=1)


def silu_slope(pre_act):
    sigmoid_value = jax.nn.sigmoid(pre_act)
    return sigmoid_value * (1.0 + pre_act * (1.0 - sigmoid_value))


def extend(source):
    padded = extended(source, (("lat", 2),), 1)
    return jnp.concatenate([padded[..., -1:], padded, padded[..., :1]], axis=3)


def stack_pair(payload, partner, upper_half):
    return jnp.where(
        upper_half, jnp.concatenate([partner, payload], 0), jnp.concatenate([payload, partner], 0)
    )


def split_pair(summed, upper_half):
    half_count = summed.shape[0] // 2
    lower_part = summed[:half_count]
    upper_part = summed[half_count:]
    return (
        jnp.where(upper_half, upper_part, lower_part),
        jnp.where(upper_half, lower_part, upper_part),
    )


def join_features(payload, state_index, low_bits, all_bits):
    for bit_index in range(low_bits, all_bits):
        partner = swapped(payload, "state", bit_index)
        payload = stack_pair(payload, partner, state_index >> bit_index & 1 == 1)
    return payload


def spread_cotangent(summed, state_index, low_bits, all_bits):
    for bit_index in reversed(range(low_bits, all_bits)):
        kept_part, sent_part = split_pair(summed, state_index >> bit_index & 1 == 1)
        summed = kept_part + swapped(sent_part, "state", bit_index)
    return summed


def spread_grads(summed, state_index, low_bits):
    for bit_index in reversed(range(low_bits)):
        kept_part, sent_part = split_pair(summed, state_index >> bit_index & 1 == 1)
        summed = kept_part + swapped(sent_part, "state", bit_index)
    return summed


def run_state(in_first, extend_fn, w_state, v_float, cot_vector, site_scale):
    stream = in_first[:, :, 1:-1, 1:-1].astype(jnp.float32)
    block_index = 0
    z_one = conv_apply(w_state[block_index, 0], make_patches(in_first))
    g_one = jax.nn.silu(z_one).astype(jnp.bfloat16)
    stream = stream + conv_apply(w_state[block_index, 1], make_patches(extend_fn(g_one)))
    saved_list = [(in_first[:, :, 1:-1, 1:-1], z_one, g_one)]
    part_row = (
        jnp.einsum("c,kcxy->k", v_float, jax.nn.silu(stream), precision=lax.Precision.HIGHEST)
        * site_scale
    )
    d_stream = (
        (cot_vector * site_scale)[:, None, None, None]
        * v_float[None, :, None, None]
        * silu_slope(stream)
    )
    grad_list = [None] * w_state.shape[0]
    for block_index in reversed(range(w_state.shape[0])):
        inner_field, z_one, g_one = saved_list[block_index]
        dz_two = d_stream.astype(jnp.bfloat16)
        cot_two = make_patches(extend_fn(dz_two))
        grad_two = grad_from(g_one, cot_two)
        dz_one = (conv_apply(flipped(w_state[block_index, 1]), cot_two) * silu_slope(z_one)).astype(
            jnp.bfloat16
        )
        cot_one = make_patches(extend_fn(dz_one))
        grad_one = grad_from(inner_field, cot_one)
        d_stream = d_stream + conv_apply(flipped(w_state[block_index, 0]), cot_one)
        grad_list[block_index] = jnp.stack([grad_one, grad_two])
    return (part_row, jnp.stack(grad_list), d_stream)


def local(spins, embed_w, block_w, readout, amp_cot):
    state_total = lax.axis_size("state")
    lat_count = lax.axis_size("lat")
    state_count = block_w.shape[0]
    group_count = state_total // state_count
    low_bits = group_count.bit_length() - 1
    all_bits = state_total.bit_length() - 1
    state_index = lax.axis_index("state")
    my_state = state_index // group_count
    my_group = state_index % group_count
    held_count = spins.shape[0]
    site_scale = 1.0 / math.sqrt(spins.shape[1] * lat_count * spins.shape[2])
    w_state = lax.dynamic_index_in_dim(block_w, my_state, 0, keepdims=False)
    v_float = lax.dynamic_index_in_dim(readout, my_state, 0, keepdims=False).astype(jnp.float32)
    cot_row = lax.dynamic_index_in_dim(amp_cot, my_state, 0, keepdims=False).reshape(
        state_count, group_count, held_count
    )
    group_pick = (jnp.arange(group_count) == my_group).astype(jnp.float32)
    group_cot = jnp.sum(cot_row * group_pick[None, :, None], axis=1).reshape(
        state_count * held_count
    )
    spin_field = spins.astype(jnp.bfloat16)[:, None]
    spin_pad = extend(spin_field)
    h_zero = conv_apply(embed_w, make_patches(spin_pad)).astype(jnp.bfloat16)
    h_pad = extend(h_zero)
    in_first = join_features(h_pad, state_index, low_bits, all_bits)
    group_row, grad_stack, d_stream = run_state(
        in_first, extend, w_state, v_float, group_cot, site_scale
    )
    own_cot_field = spread_cotangent(d_stream, state_index, low_bits, all_bits)
    contrib = spin_contract(own_cot_field, spin_pad)
    state_pick = (jnp.arange(state_count) == my_state).astype(jnp.float32)
    spread_row = (
        group_row.reshape(state_count, 1, held_count) * group_pick[None, :, None]
    ).reshape(-1)
    amp_part = state_pick[:, None] * spread_row[None, :]
    log_amp, embed_grad = lax.psum((amp_part, contrib), ("state", "lat"))
    by_channel = jnp.transpose(grad_stack, (2, 0, 1, 3))
    own_rows = spread_grads(by_channel, state_index, low_bits)
    block_grad = lax.psum(own_rows, "lat")
    return (log_amp, block_grad, embed_grad)


def solution(mesh):
    return jax.shard_map(
        local,
        mesh=mesh,
        in_specs=(P("state", "lat", None), P(), P(), P(), P()),
        out_specs=(P(), P("state", None, None, None), P()),
        check_vma=False,
    )
```

profile of v0, /device:TPU:1, one launch (start us, length us, event | category | flops | bytes accessed | tf_op | source)
XLA Modules:
  0.0 407.7 jit_solution(13275533866061689292)
XLA Ops:
  8.0 8.8 %collective-permute-start.1 = (bf16[1,1,1,128]{3,2,1,0:T(2,128)(2,1)S(1)}, bf16[1,1,1,128]{3,2,1,0:T(2,128)(2,1)S(1)}, u32[]{:S(2)}, u32[]{:S(2)}) collective-permute-start(bf16[1,1,1,128]{3,2,1,0:T(2,128)(2,1)S(1)} %convert_bitcast_fusion), channel_id=1, source_target_pairs={{1,0},{2,1},{3,2},{4,3},{5,4},{6,5},{7,6},{0,7},{9,8},{10,9},{11,1... | collective-permute-start | bytes 776 | tf_op jit(solution)/shard_map/ppermute | solution.py:17
  25.2 5.6 %collective-permute-start.3 = (bf16[1,64,1,128]{3,1,2,0:T(8,128)(2,1)S(1)}, bf16[1,64,1,128]{3,1,2,0:T(8,128)(2,1)S(1)}, u32[]{:S(2)}, u32[]{:S(2)}) collective-permute-start(bf16[1,64,1,128]{3,1,2,0:T(8,128)(2,1)S(1)} %fusion.29), channel_id=1, source_target_pairs={{1,0},{2,1},{3,2},{4,3},{5,4},{6,5},{7,6},{0,7},{9,8},{10,9},{11,1... | collective-permute-start | bytes 49160 | tf_op jit(solution)/shard_map/ppermute | solution.py:17
  36.0 3.4 collective-permute-done.4
  39.6 4.1 %collective-permute-start.5 = (bf16[2,64,3,130]{3,1,2,0:T(8,128)(2,1)S(1)}, bf16[2,64,3,130]{3,1,2,0:T(8,128)(2,1)S(1)}, u32[]{:S(2)}, u32[]{:S(2)}) collective-permute-start(bf16[2,64,3,130]{3,1,2,0:T(8,128)(2,1)S(1)} %maximum_select_fusion.3), channel_id=1, source_target_pairs={{0,64},{8,72},{16,80},{24,88},{32,96},{40,104},{48,112},{56,120},{... | collective-permute-start | bytes 299528 | tf_op jit(solution)/shard_map/ppermute | solution.py:25
  44.5 4.5 %collective-permute-done.5 = bf16[2,64,3,130]{3,1,2,0:T(8,128)(2,1)S(1)} collective-permute-done((bf16[2,64,3,130]{3,1,2,0:T(8,128)(2,1)S(1)}, bf16[2,64,3,130]{3,1,2,0:T(8,128)(2,1)S(1)}, u32[]{:S(2)}, u32[]{:S(2)}) %collective-permute-start.5) | collective-permute-done | bytes 99872 | tf_op jit(solution)/shard_map/ppermute | solution.py:25
  49.2 8.3 %collective-permute-start.6 = (bf16[4,64,3,130]{3,1,2,0:T(8,128)(2,1)S(1)}, bf16[4,64,3,130]{3,1,2,0:T(8,128)(2,1)S(1)}, u32[]{:S(2)}, u32[]{:S(2)}) collective-permute-start(bf16[4,64,3,130]{3,1,2,0:T(8,128)(2,1)S(1)} %maximum_select_fusion.2), channel_id=1, source_target_pairs={{0,128},{8,136},{16,144},{24,152},{32,160},{40,168},{48,176},{56,1... | collective-permute-start | bytes 599048 | tf_op jit(solution)/shard_map/ppermute | solution.py:25
  58.0 7.0 %collective-permute-done.6 = bf16[4,64,3,130]{3,1,2,0:T(8,128)(2,1)S(1)} collective-permute-done((bf16[4,64,3,130]{3,1,2,0:T(8,128)(2,1)S(1)}, bf16[4,64,3,130]{3,1,2,0:T(8,128)(2,1)S(1)}, u32[]{:S(2)}, u32[]{:S(2)}) %collective-permute-start.6) | collective-permute-done | bytes 199712 | tf_op jit(solution)/shard_map/ppermute | solution.py:25
  65.3 4.8 %collective-permute-start.7 = (bf16[8,64,3,130]{3,1,2,0:T(8,128)(2,1)S(1)}, bf16[8,64,3,130]{3,1,2,0:T(8,128)(2,1)}, u32[]{:S(2)}, u32[]{:S(2)}) collective-permute-start(bf16[8,64,3,130]{3,1,2,0:T(8,128)(2,1)S(1)} %maximum_select_fusion.1), channel_id=1, source_target_pairs={{0,256},{8,264},{16,272},{24,280},{32,288},{40,296},{48,304},{56,3... | collective-permute-start | bytes 1198088 | tf_op jit(solution)/shard_map/ppermute | solution.py:25
  71.3 11.7 %collective-permute-done.7 = bf16[8,64,3,130]{3,1,2,0:T(8,128)(2,1)} collective-permute-done((bf16[8,64,3,130]{3,1,2,0:T(8,128)(2,1)S(1)}, bf16[8,64,3,130]{3,1,2,0:T(8,128)(2,1)}, u32[]{:S(2)}, u32[]{:S(2)}) %collective-permute-start.7) | collective-permute-done | bytes 399392 | tf_op jit(solution)/shard_map/ppermute | solution.py:25
  87.9 10.2 %collective-permute-start.9 = (bf16[16,64,1,128]{3,1,2,0:T(8,128)(2,1)S(1)}, bf16[16,64,1,128]{3,1,2,0:T(8,128)(2,1)S(1)}, u32[]{:S(2)}, u32[]{:S(2)}) collective-permute-start(bf16[16,64,1,128]{3,1,2,0:T(8,128)(2,1)S(1)} %get-tuple-element.37), channel_id=1, source_target_pairs={{1,0},{2,1},{3,2},{4,3},{5,4},{6,5},{7,6},{0,7},{9,8},{10,9},{11,1... | collective-permute-start | bytes 786440 | tf_op jit(solution)/shard_map/ppermute | solution.py:17
  98.1 23.5 %collective-permute-start.8 = (bf16[16,64,1,128]{3,1,2,0:T(8,128)(2,1)S(1)}, bf16[16,64,1,128]{3,1,2,0:T(8,128)(2,1)S(1)}, u32[]{:S(2)}, u32[]{:S(2)}) collective-permute-start(bf16[16,64,1,128]{3,1,2,0:T(8,128)(2,1)S(1)} %get-tuple-element.37), channel_id=1, source_target_pairs={{0,1},{1,2},{2,3},{3,4},{4,5},{5,6},{6,7},{7,0},{8,9},{9,10},{10,1... | collective-permute-start | bytes 786440 | tf_op jit(solution)/shard_map/ppermute | solution.py:14
  127.8 3.1 fusion.67
  130.9 5.1 %collective-permute-start.11 = (bf16[16,64,1,128]{3,1,2,0:T(8,128)(2,1)S(1)}, bf16[16,64,1,128]{3,1,2,0:T(8,128)(2,1)S(1)}, u32[]{:S(2)}, u32[]{:S(2)}) collective-permute-start(bf16[16,64,1,128]{3,1,2,0:T(8,128)(2,1)S(1)} %get-tuple-element.23), channel_id=1, source_target_pairs={{1,0},{2,1},{3,2},{4,3},{5,4},{6,5},{7,6},{0,7},{9,8},{10,9},{11,1... | collective-permute-start | bytes 786440 | tf_op jit(solution)/shard_map/ppermute | solution.py:17
  152.5 2.4 collective-permute-start.13
  154.9 3.3 collective-permute-start.12
  161.6 2.5 collective-permute-done.12
  174.5 4.6 %collective-permute-start.14 = (f32[32,1,2,576]{3,0,2,1:T(8,128)}, f32[32,1,2,576]{3,0,2,1:T(8,128)S(1)}, u32[]{:S(2)}, u32[]{:S(2)}) collective-permute-start(f32[32,1,2,576]{3,0,2,1:T(8,128)} %copy.28), channel_id=1, source_target_pairs={{0,16},{8,24},{16,0},{24,8},{32,48},{40,56},{48,32},{56,40},{64,80... | collective-permute-start | bytes 442376 | tf_op jit(solution)/shard_map/ppermute | solution.py:25
  179.2 2.6 fusion.20
  182.5 7.1 %collective-permute-start.16 = (f32[8,64,1,128]{3,1,2,0:T(8,128)S(1)}, f32[8,64,1,128]{3,1,2,0:T(8,128)}, u32[]{:S(2)}, u32[]{:S(2)}) collective-permute-start(f32[8,64,1,128]{3,1,2,0:T(8,128)S(1)} %slice_select_fusion.2), channel_id=1, source_target_pairs={{0,256},{8,264},{16,272},{24,280},{32,288},{40,296},{48,304},{56,3... | collective-permute-start | bytes 786440 | tf_op jit(solution)/shard_map/ppermute | solution.py:25
  196.9 4.2 %collective-permute-done.16 = f32[8,64,1,128]{3,1,2,0:T(8,128)} collective-permute-done((f32[8,64,1,128]{3,1,2,0:T(8,128)S(1)}, f32[8,64,1,128]{3,1,2,0:T(8,128)}, u32[]{:S(2)}, u32[]{:S(2)}) %collective-permute-start.16) | collective-permute-done | bytes 262176 | tf_op jit(solution)/shard_map/ppermute | solution.py:25
  202.9 6.2 %collective-permute-start.17 = (f32[4,64,1,128]{3,1,2,0:T(8,128)}, f32[4,64,1,128]{3,1,2,0:T(8,128)}, u32[]{:S(2)}, u32[]{:S(2)}) collective-permute-start(f32[4,64,1,128]{3,1,2,0:T(8,128)} %slice_select_fusion.3), channel_id=1, source_target_pairs={{0,128},{8,136},{16,144},{24,152},{32,160},{40,168},{48,176},{56,1... | collective-permute-start | bytes 393224 | tf_op jit(solution)/shard_map/ppermute | solution.py:25
  216.8 5.6 %collective-permute-start.18 = (f32[2,64,1,128]{3,1,2,0:T(8,128)S(1)}, f32[2,64,1,128]{3,1,2,0:T(8,128)S(1)}, u32[]{:S(2)}, u32[]{:S(2)}) collective-permute-start(f32[2,64,1,128]{3,1,2,0:T(8,128)S(1)} %slice_select_fusion.4), channel_id=1, source_target_pairs={{0,64},{8,72},{16,80},{24,88},{32,96},{40,104},{48,112},{56,120},{... | collective-permute-start | bytes 196616 | tf_op jit(solution)/shard_map/ppermute | solution.py:25
  226.6 69.0 %all-reduce.3.cloned.1.call-done = f32[16,1,2,576]{0,3,2,1:T(8,128)} async-done(((f32[16,1,2,576]{0,3,2,1:T(8,128)}), f32[16,1,2,576]{0,3,2,1:T(8,128)}) %all-reduce.3.cloned.1.call-update) | async-done | bytes 73744 | tf_op jit(solution)/shard_map/psum | solution.py:192
  299.1 101.8 %all-reduce = (f32[16,64]{1,0:T(8,128)}, f32[64,9]{0,1:T(8,128)}) all-reduce(f32[16,64]{1,0:T(8,128)S(1)} %broadcast_multiply_fusion.1, f32[64,9]{0,1:T(8,128)S(1)} %stack.47), channel_id=1, replica_groups=mesh['state'=64,'lat'=8] {'state','lat'}, use_global_device_ids=true, to_apply=%region_1.2 | all-reduce | flops 1600 | bytes 12800 | tf_op jit(solution)/shard_map/psum | solution.py:189
  (201 shorter events, 83.4 us)
Async XLA Ops:
  7.2 288.5 %all-reduce.3.cloned.1.call-start = ((), (), s32[]{:S(2)}) async-start(), calls=%async_computation | async-start | bytes 1179648 | tf_op jit(solution)/shard_map/psum | solution.py:192
  8.0 10.7 %collective-permute-start.1 = (bf16[1,1,1,128]{3,2,1,0:T(2,128)(2,1)S(1)}, bf16[1,1,1,128]{3,2,1,0:T(2,128)(2,1)S(1)}, u32[]{:S(2)}, u32[]{:S(2)}) collective-permute-start(bf16[1,1,1,128]{3,2,1,0:T(2,128)(2,1)S(1)} %convert_bitcast_fusion), channel_id=1, source_target_pairs={{1,0},{2,1},{3,2},{4,3},{5,4},{6,5},{7,6},{0,7},{9,8},{10,9},{11,1... | collective-permute-start | bytes 776 | tf_op jit(solution)/shard_map/ppermute | solution.py:17
  16.8 3.0 collective-permute-start
  25.2 7.5 %collective-permute-start.3 = (bf16[1,64,1,128]{3,1,2,0:T(8,128)(2,1)S(1)}, bf16[1,64,1,128]{3,1,2,0:T(8,128)(2,1)S(1)}, u32[]{:S(2)}, u32[]{:S(2)}) collective-permute-start(bf16[1,64,1,128]{3,1,2,0:T(8,128)(2,1)S(1)} %fusion.29), channel_id=1, source_target_pairs={{1,0},{2,1},{3,2},{4,3},{5,4},{6,5},{7,6},{0,7},{9,8},{10,9},{11,1... | collective-permute-start | bytes 49160 | tf_op jit(solution)/shard_map/ppermute | solution.py:17
  30.8 3.1 collective-permute-start.2
  34.1 5.4 %collective-permute-start.4 = (bf16[1,64,3,130]{3,1,2,0:T(8,128)(2,1)S(1)}, bf16[1,64,3,130]{3,1,2,0:T(8,128)(2,1)S(1)}, u32[]{:S(2)}, u32[]{:S(2)}) collective-permute-start(bf16[1,64,3,130]{3,1,2,0:T(8,128)(2,1)S(1)} %pad_maximum_fusion.21), channel_id=1, source_target_pairs={{0,32},{8,40},{16,48},{24,56},{32,0},{40,8},{48,16},{56,24},{64,96... | collective-permute-start | bytes 149768 | tf_op jit(solution)/shard_map/ppermute | solution.py:25
  39.6 9.4 %collective-permute-start.5 = (bf16[2,64,3,130]{3,1,2,0:T(8,128)(2,1)S(1)}, bf16[2,64,3,130]{3,1,2,0:T(8,128)(2,1)S(1)}, u32[]{:S(2)}, u32[]{:S(2)}) collective-permute-start(bf16[2,64,3,130]{3,1,2,0:T(8,128)(2,1)S(1)} %maximum_select_fusion.3), channel_id=1, source_target_pairs={{0,64},{8,72},{16,80},{24,88},{32,96},{40,104},{48,112},{56,120},{... | collective-permute-start | bytes 299528 | tf_op jit(solution)/shard_map/ppermute | solution.py:25
  49.2 15.8 %collective-permute-start.6 = (bf16[4,64,3,130]{3,1,2,0:T(8,128)(2,1)S(1)}, bf16[4,64,3,130]{3,1,2,0:T(8,128)(2,1)S(1)}, u32[]{:S(2)}, u32[]{:S(2)}) collective-permute-start(bf16[4,64,3,130]{3,1,2,0:T(8,128)(2,1)S(1)} %maximum_select_fusion.2), channel_id=1, source_target_pairs={{0,128},{8,136},{16,144},{24,152},{32,160},{40,168},{48,176},{56,1... | collective-permute-start | bytes 599048 | tf_op jit(solution)/shard_map/ppermute | solution.py:25
  65.3 17.7 %collective-permute-start.7 = (bf16[8,64,3,130]{3,1,2,0:T(8,128)(2,1)S(1)}, bf16[8,64,3,130]{3,1,2,0:T(8,128)(2,1)}, u32[]{:S(2)}, u32[]{:S(2)}) collective-permute-start(bf16[8,64,3,130]{3,1,2,0:T(8,128)(2,1)S(1)} %maximum_select_fusion.1), channel_id=1, source_target_pairs={{0,256},{8,264},{16,272},{24,280},{32,288},{40,296},{48,304},{56,3... | collective-permute-start | bytes 1198088 | tf_op jit(solution)/shard_map/ppermute | solution.py:25
  87.9 36.7 %collective-permute-start.9 = (bf16[16,64,1,128]{3,1,2,0:T(8,128)(2,1)S(1)}, bf16[16,64,1,128]{3,1,2,0:T(8,128)(2,1)S(1)}, u32[]{:S(2)}, u32[]{:S(2)}) collective-permute-start(bf16[16,64,1,128]{3,1,2,0:T(8,128)(2,1)S(1)} %get-tuple-element.37), channel_id=1, source_target_pairs={{1,0},{2,1},{3,2},{4,3},{5,4},{6,5},{7,6},{0,7},{9,8},{10,9},{11,1... | collective-permute-start | bytes 786440 | tf_op jit(solution)/shard_map/ppermute | solution.py:17
  98.1 27.3 %collective-permute-start.8 = (bf16[16,64,1,128]{3,1,2,0:T(8,128)(2,1)S(1)}, bf16[16,64,1,128]{3,1,2,0:T(8,128)(2,1)S(1)}, u32[]{:S(2)}, u32[]{:S(2)}) collective-permute-start(bf16[16,64,1,128]{3,1,2,0:T(8,128)(2,1)S(1)} %get-tuple-element.37), channel_id=1, source_target_pairs={{0,1},{1,2},{2,3},{3,4},{4,5},{5,6},{6,7},{7,0},{8,9},{9,10},{10,1... | collective-permute-start | bytes 786440 | tf_op jit(solution)/shard_map/ppermute | solution.py:14
  130.9 14.5 %collective-permute-start.11 = (bf16[16,64,1,128]{3,1,2,0:T(8,128)(2,1)S(1)}, bf16[16,64,1,128]{3,1,2,0:T(8,128)(2,1)S(1)}, u32[]{:S(2)}, u32[]{:S(2)}) collective-permute-start(bf16[16,64,1,128]{3,1,2,0:T(8,128)(2,1)S(1)} %get-tuple-element.23), channel_id=1, source_target_pairs={{1,0},{2,1},{3,2},{4,3},{5,4},{6,5},{7,6},{0,7},{9,8},{10,9},{11,1... | collective-permute-start | bytes 786440 | tf_op jit(solution)/shard_map/ppermute | solution.py:17
  136.0 9.4 %collective-permute-start.10 = (bf16[16,64,1,128]{3,1,2,0:T(8,128)(2,1)S(1)}, bf16[16,64,1,128]{3,1,2,0:T(8,128)(2,1)}, u32[]{:S(2)}, u32[]{:S(2)}) collective-permute-start(bf16[16,64,1,128]{3,1,2,0:T(8,128)(2,1)S(1)} %get-tuple-element.23), channel_id=1, source_target_pairs={{0,1},{1,2},{2,3},{3,4},{4,5},{5,6},{6,7},{7,0},{8,9},{9,10},{10,1... | collective-permute-start | bytes 786440 | tf_op jit(solution)/shard_map/ppermute | solution.py:14
  152.5 9.1 %collective-permute-start.13 = (bf16[16,64,1,128]{3,1,2,0:T(8,128)(2,1)S(1)}, bf16[16,64,1,128]{3,1,2,0:T(8,128)(2,1)S(1)}, u32[]{:S(2)}, u32[]{:S(2)}) collective-permute-start(bf16[16,64,1,128]{3,1,2,0:T(8,128)(2,1)S(1)} %fusion.26), channel_id=1, source_target_pairs={{1,0},{2,1},{3,2},{4,3},{5,4},{6,5},{7,6},{0,7},{9,8},{10,9},{11,1... | collective-permute-start | bytes 786440 | tf_op jit(solution)/shard_map/ppermute | solution.py:17
  154.9 9.2 %collective-permute-start.12 = (bf16[16,64,1,128]{3,1,2,0:T(8,128)(2,1)S(1)}, bf16[16,64,1,128]{3,1,2,0:T(8,128)(2,1)}, u32[]{:S(2)}, u32[]{:S(2)}) collective-permute-start(bf16[16,64,1,128]{3,1,2,0:T(8,128)(2,1)S(1)} %fusion.26), channel_id=1, source_target_pairs={{0,1},{1,2},{2,3},{3,4},{4,5},{5,6},{6,7},{7,0},{8,9},{9,10},{10,1... | collective-permute-start | bytes 786440 | tf_op jit(solution)/shard_map/ppermute | solution.py:14
  174.5 15.2 %collective-permute-start.14 = (f32[32,1,2,576]{3,0,2,1:T(8,128)}, f32[32,1,2,576]{3,0,2,1:T(8,128)S(1)}, u32[]{:S(2)}, u32[]{:S(2)}) collective-permute-start(f32[32,1,2,576]{3,0,2,1:T(8,128)} %copy.28), channel_id=1, source_target_pairs={{0,16},{8,24},{16,0},{24,8},{32,48},{40,56},{48,32},{56,40},{64,80... | collective-permute-start | bytes 442376 | tf_op jit(solution)/shard_map/ppermute | solution.py:25
  182.5 18.6 %collective-permute-start.16 = (f32[8,64,1,128]{3,1,2,0:T(8,128)S(1)}, f32[8,64,1,128]{3,1,2,0:T(8,128)}, u32[]{:S(2)}, u32[]{:S(2)}) collective-permute-start(f32[8,64,1,128]{3,1,2,0:T(8,128)S(1)} %slice_select_fusion.2), channel_id=1, source_target_pairs={{0,256},{8,264},{16,272},{24,280},{32,288},{40,296},{48,304},{56,3... | collective-permute-start | bytes 786440 | tf_op jit(solution)/shard_map/ppermute | solution.py:25
  194.7 18.5 %collective-permute-start.15 = (f32[16,1,2,576]{3,0,2,1:T(8,128)S(1)}, f32[16,1,2,576]{3,0,2,1:T(8,128)}, u32[]{:S(2)}, u32[]{:S(2)}) collective-permute-start(f32[16,1,2,576]{3,0,2,1:T(8,128)S(1)} %copy.30), channel_id=1, source_target_pairs={{0,8},{8,0},{16,24},{24,16},{32,40},{40,32},{48,56},{56,48},{64,72... | collective-permute-start | bytes 221192 | tf_op jit(solution)/shard_map/ppermute | solution.py:25
  202.9 12.2 %collective-permute-start.17 = (f32[4,64,1,128]{3,1,2,0:T(8,128)}, f32[4,64,1,128]{3,1,2,0:T(8,128)}, u32[]{:S(2)}, u32[]{:S(2)}) collective-permute-start(f32[4,64,1,128]{3,1,2,0:T(8,128)} %slice_select_fusion.3), channel_id=1, source_target_pairs={{0,128},{8,136},{16,144},{24,152},{32,160},{40,168},{48,176},{56,1... | collective-permute-start | bytes 393224 | tf_op jit(solution)/shard_map/ppermute | solution.py:25
  215.2 82.5 %copy-start.19 = (bf16[1,1,1,128]{3,2,1,0:T(2,128)(2,1)S(1)}, bf16[1,1,1,128]{3,2,1,0:T(2,128)(2,1)}, u32[]{:S(2)}) copy-start(bf16[1,1,1,128]{3,2,1,0:T(2,128)(2,1)} %get-tuple-element.20) | copy-start | bytes 772
  215.2 82.7 %copy-start.20 = (bf16[1,1,1,128]{3,2,1,0:T(2,128)(2,1)S(1)}, bf16[1,1,1,128]{3,2,1,0:T(2,128)(2,1)}, u32[]{:S(2)}) copy-start(bf16[1,1,1,128]{3,2,1,0:T(2,128)(2,1)} %get-tuple-element.18) | copy-start | bytes 772
  215.2 82.9 %copy-start.21 = (bf16[1,1,1,128]{3,2,1,0:T(2,128)(2,1)S(1)}, bf16[1,1,1,128]{3,2,1,0:T(2,128)(2,1)}, u32[]{:S(2)}) copy-start(bf16[1,1,1,128]{3,2,1,0:T(2,128)(2,1)} %get-tuple-element.16) | copy-start | bytes 772
  216.8 7.7 %collective-permute-start.18 = (f32[2,64,1,128]{3,1,2,0:T(8,128)S(1)}, f32[2,64,1,128]{3,1,2,0:T(8,128)S(1)}, u32[]{:S(2)}, u32[]{:S(2)}) collective-permute-start(f32[2,64,1,128]{3,1,2,0:T(8,128)S(1)} %slice_select_fusion.4), channel_id=1, source_target_pairs={{0,64},{8,72},{16,80},{24,88},{32,96},{40,104},{48,112},{56,120},{... | collective-permute-start | bytes 196616 | tf_op jit(solution)/shard_map/ppermute | solution.py:25
  224.6 72.9 %collective-permute-start.19 = (f32[1,64,1,128]{3,1,2,0:T(8,128)S(1)}, f32[1,64,1,128]{3,1,2,0:T(8,128)S(1)}, u32[]{:S(2)}, u32[]{:S(2)}) collective-permute-start(f32[1,64,1,128]{3,1,2,0:T(8,128)S(1)} %slice_select_fusion.5), channel_id=1, source_target_pairs={{0,32},{8,40},{16,48},{24,56},{32,0},{40,8},{48,16},{56,24},{64,96... | collective-permute-start | bytes 98312 | tf_op jit(solution)/shard_map/ppermute | solution.py:25
  (26 other events, 659.2 us)
Sparse Core Ops, SparseCore 0:
  224.7 70.9 all-reduce.2
where the time goes:
time: 409 us; the launch traced here: 408 us
  starting transfers between devices  111 us (27%)
  waiting for transfers between devices  105 us (26%)
  blocking collectives  102 us (25%)
  other arithmetic  30.2 us (7%)
  local copies, waits for them, and re-layouts  30 us (7%)
  between operations  15 us (4%)
  matrix products  13.8 us (3%)
    psum x1, blocking collectives, local(): log_amp, embed_grad = lax.psum((amp_part, contrib), ('state', 'lat'))  102 us
    psum x1, waiting for transfers between devices, local(): block_grad = lax.psum(own_rows, 'lat')  69 us
    ppermute x10, starting transfers between devices, swapped(): return lax.ppermute(value, axis, pairs)  46.8 us
    ppermute x5, starting transfers between devices, extended(): lax.ppermute(lax.slice_in_dim(block, block.shape[dim] - width, None, axis...  32.6 us
    ppermute x5, starting transfers between devices, extended(): lax.ppermute(lax.slice_in_dim(block, 0, width, axis=dim), axis, backward)  32 us
    ppermute x10, waiting for transfers between devices, swapped(): return lax.ppermute(value, axis, pairs)  30.8 us
    unnamed x21, other arithmetic  10.9 us
    unnamed x78, local copies, waits for them, and re-layouts  9.08 us
  transfers between devices with their start and end apart: 21, of which 10 were waited for; matrix products, arithmetic and copies ran while one was open for 9% of the time, Pallas kernels for 0%

commit v1 on v0

--- a/solution.py
+++ b/solution.py
@@ -189,7 +189,8 @@
     log_amp, embed_grad = lax.psum((amp_part, contrib), ("state", "lat"))
     by_channel = jnp.transpose(grad_stack, (2, 0, 1, 3))
     own_rows = spread_grads(by_channel, state_index, low_bits)
-    block_grad = lax.psum(own_rows, "lat")
+    blocks = lax.all_gather(own_rows, "lat", axis=0, tiled=False)
+    block_grad = blocks.sum(axis=0)
     return (log_amp, block_grad, embed_grad)
 
 

time: 409 us -> 333 us (0.81)
  waiting for transfers between devices: 105 us -> 63.5 us
  between operations: 15 us -> 1.63 us
  local copies, waits for them, and re-layouts: 30 us -> 18.6 us
  blocking collectives: 102 us -> 113 us
  starting transfers between devices: 111 us -> 101 us
  other arithmetic: 30.2 us -> 21.6 us
    psum x1 -> x0, waiting for transfers between devices: 69 us -> none  [local(): block_grad = lax.psum(own_rows, 'lat')]
    ppermute x5, starting transfers between devices: 32.6 us -> 11 us  [extended(): lax.ppermute(lax.slice_in_dim(block, block.shape[dim] - width, None, axis...]
    all_gather x0 -> x1, blocking collectives: none -> 16.9 us  [local(): blocks = lax.all_gather(own_rows, 'lat', axis=0, tiled=False)]
    ppermute x10, waiting for transfers between devices: 30.8 us -> 41.3 us  [swapped(): return lax.ppermute(value, axis, pairs)]
    ppermute x5, waiting for transfers between devices: 0.01 us -> 10.1 us  [extended(): lax.ppermute(lax.slice_in_dim(block, 0, width, axis=dim), axis, backward)]
    ppermute x10, starting transfers between devices: 46.8 us -> 54.1 us  [swapped(): return lax.ppermute(value, axis, pairs)]
    ppermute x5, waiting for transfers between devices: 5.53 us -> 12.1 us  [extended(): lax.ppermute(lax.slice_in_dim(block, block.shape[dim] - width, None, axis...]
    psum x1, blocking collectives: 102 us -> 95.9 us  [local(): log_amp, embed_grad = lax.psum((amp_part, contrib), ('state', 'lat'))]
  transfers between devices with their start and end apart: 21 -> 20, of which waited for: 10 -> 12; matrix products, arithmetic and copies ran while one was open for 9% -> 6% of each run, Pallas kernels for 0% -> 0%
where the time goes in v1:
time: 333 us; the launch traced here: 331 us
  blocking collectives  113 us (34%)
  starting transfers between devices  101 us (30%)
  waiting for transfers between devices  63.5 us (19%)
  other arithmetic  21.6 us (6%)
  local copies, waits for them, and re-layouts  18.6 us (6%)
  matrix products  12.9 us (4%)
    psum x1, blocking collectives, local(): log_amp, embed_grad = lax.psum((amp_part, contrib), ('state', 'lat'))  95.9 us
    ppermute x10, starting transfers between devices, swapped(): return lax.ppermute(value, axis, pairs)  54.1 us
    ppermute x10, waiting for transfers between devices, swapped(): return lax.ppermute(value, axis, pairs)  41.3 us
    ppermute x5, starting transfers between devices, extended(): lax.ppermute(lax.slice_in_dim(block, 0, width, axis=dim), axis, backward)  35.4 us
    all_gather x1, blocking collectives, local(): blocks = lax.all_gather(own_rows, 'lat', axis=0, tiled=False)  16.9 us
    ppermute x5, waiting for transfers between devices, extended(): lax.ppermute(lax.slice_in_dim(block, block.shape[dim] - width, None, axis...  12.1 us
    unnamed x22, other arithmetic  11.9 us
    ppermute x5, starting transfers between devices, extended(): lax.ppermute(lax.slice_in_dim(block, block.shape[dim] - width, None, axis...  11 us
  transfers between devices with their start and end apart: 20, of which 12 were waited for; matrix products, arithmetic and copies ran while one was open for 6% of the time, Pallas kernels for 0%

profile of v1, /device:TPU:1, one launch (start us, length us, event | category | flops | bytes accessed | tf_op | source)
XLA Modules:
  0.0 331.5 jit_solution(3775132777399737404)
XLA Ops:
  1.5 8.8 %collective-permute-start.1 = (bf16[1,1,1,128]{3,2,1,0:T(2,128)(2,1)S(1)}, bf16[1,1,1,128]{3,2,1,0:T(2,128)(2,1)S(1)}, u32[]{:S(2)}, u32[]{:S(2)}) collective-permute-start(bf16[1,1,1,128]{3,2,1,0:T(2,128)(2,1)S(1)} %convert_bitcast_fusion), channel_id=1, source_target_pairs={{1,0},{2,1},{3,2},{4,3},{5,4},{6,5},{7,6},{0,7},{9,8},{10,9},{11,1... | collective-permute-start | bytes 776 | tf_op jit(solution)/shard_map/ppermute | solution.py:17
  18.8 5.6 %collective-permute-start.3 = (bf16[1,64,1,128]{3,1,2,0:T(8,128)(2,1)S(1)}, bf16[1,64,1,128]{3,1,2,0:T(8,128)(2,1)S(1)}, u32[]{:S(2)}, u32[]{:S(2)}) collective-permute-start(bf16[1,64,1,128]{3,1,2,0:T(8,128)(2,1)S(1)} %fusion.29), channel_id=1, source_target_pairs={{1,0},{2,1},{3,2},{4,3},{5,4},{6,5},{7,6},{0,7},{9,8},{10,9},{11,1... | collective-permute-start | bytes 49160 | tf_op jit(solution)/shard_map/ppermute | solution.py:17
  29.6 3.4 %collective-permute-done.4 = bf16[1,64,3,130]{3,1,2,0:T(8,128)(2,1)S(1)} collective-permute-done((bf16[1,64,3,130]{3,1,2,0:T(8,128)(2,1)S(1)}, bf16[1,64,3,130]{3,1,2,0:T(8,128)(2,1)S(1)}, u32[]{:S(2)}, u32[]{:S(2)}) %collective-permute-start.4) | collective-permute-done | bytes 49952 | tf_op jit(solution)/shard_map/ppermute | solution.py:25
  33.1 4.1 %collective-permute-start.5 = (bf16[2,64,3,130]{3,1,2,0:T(8,128)(2,1)S(1)}, bf16[2,64,3,130]{3,1,2,0:T(8,128)(2,1)}, u32[]{:S(2)}, u32[]{:S(2)}) collective-permute-start(bf16[2,64,3,130]{3,1,2,0:T(8,128)(2,1)S(1)} %maximum_select_fusion.3), channel_id=1, source_target_pairs={{0,64},{8,72},{16,80},{24,88},{32,96},{40,104},{48,112},{56,120},{... | collective-permute-start | bytes 299528 | tf_op jit(solution)/shard_map/ppermute | solution.py:25
  38.4 4.3 %collective-permute-done.5 = bf16[2,64,3,130]{3,1,2,0:T(8,128)(2,1)} collective-permute-done((bf16[2,64,3,130]{3,1,2,0:T(8,128)(2,1)S(1)}, bf16[2,64,3,130]{3,1,2,0:T(8,128)(2,1)}, u32[]{:S(2)}, u32[]{:S(2)}) %collective-permute-start.5) | collective-permute-done | bytes 99872 | tf_op jit(solution)/shard_map/ppermute | solution.py:25
  43.8 8.3 %collective-permute-start.6 = (bf16[4,64,3,130]{3,1,2,0:T(8,128)(2,1)S(1)}, bf16[4,64,3,130]{3,1,2,0:T(8,128)(2,1)S(1)}, u32[]{:S(2)}, u32[]{:S(2)}) collective-permute-start(bf16[4,64,3,130]{3,1,2,0:T(8,128)(2,1)S(1)} %maximum_select_fusion.2), channel_id=1, source_target_pairs={{0,128},{8,136},{16,144},{24,152},{32,160},{40,168},{48,176},{56,1... | collective-permute-start | bytes 599048 | tf_op jit(solution)/shard_map/ppermute | solution.py:25
  52.2 7.4 %collective-permute-done.6 = bf16[4,64,3,130]{3,1,2,0:T(8,128)(2,1)S(1)} collective-permute-done((bf16[4,64,3,130]{3,1,2,0:T(8,128)(2,1)S(1)}, bf16[4,64,3,130]{3,1,2,0:T(8,128)(2,1)S(1)}, u32[]{:S(2)}, u32[]{:S(2)}) %collective-permute-start.6) | collective-permute-done | bytes 199712 | tf_op jit(solution)/shard_map/ppermute | solution.py:25
  59.9 4.8 %collective-permute-start.7 = (bf16[8,64,3,130]{3,1,2,0:T(8,128)(2,1)S(1)}, bf16[8,64,3,130]{3,1,2,0:T(8,128)(2,1)S(1)}, u32[]{:S(2)}, u32[]{:S(2)}) collective-permute-start(bf16[8,64,3,130]{3,1,2,0:T(8,128)(2,1)S(1)} %maximum_select_fusion.1), channel_id=1, source_target_pairs={{0,256},{8,264},{16,272},{24,280},{32,288},{40,296},{48,304},{56,3... | collective-permute-start | bytes 1198088 | tf_op jit(solution)/shard_map/ppermute | solution.py:25
  65.4 12.0 %collective-permute-done.7 = bf16[8,64,3,130]{3,1,2,0:T(8,128)(2,1)S(1)} collective-permute-done((bf16[8,64,3,130]{3,1,2,0:T(8,128)(2,1)S(1)}, bf16[8,64,3,130]{3,1,2,0:T(8,128)(2,1)S(1)}, u32[]{:S(2)}, u32[]{:S(2)}) %collective-permute-start.7) | collective-permute-done | bytes 399392 | tf_op jit(solution)/shard_map/ppermute | solution.py:25
  80.9 10.2 %collective-permute-start.9 = (bf16[16,64,1,128]{3,1,2,0:T(8,128)(2,1)S(1)}, bf16[16,64,1,128]{3,1,2,0:T(8,128)(2,1)S(1)}, u32[]{:S(2)}, u32[]{:S(2)}) collective-permute-start(bf16[16,64,1,128]{3,1,2,0:T(8,128)(2,1)S(1)} %get-tuple-element.37), channel_id=1, source_target_pairs={{1,0},{2,1},{3,2},{4,3},{5,4},{6,5},{7,6},{0,7},{9,8},{10,9},{11,1... | collective-permute-start | bytes 786440 | tf_op jit(solution)/shard_map/ppermute | solution.py:17
  93.9 10.1 %collective-permute-done.9 = bf16[16,64,1,128]{3,1,2,0:T(8,128)(2,1)S(1)} collective-permute-done((bf16[16,64,1,128]{3,1,2,0:T(8,128)(2,1)S(1)}, bf16[16,64,1,128]{3,1,2,0:T(8,128)(2,1)S(1)}, u32[]{:S(2)}, u32[]{:S(2)}) %collective-permute-start.9) | collective-permute-done | bytes 262176 | tf_op jit(solution)/shard_map/ppermute | solution.py:17
  104.0 9.2 %collective-permute-done.8 = bf16[16,64,1,128]{3,1,2,0:T(8,128)(2,1)S(1)} collective-permute-done((bf16[16,64,1,128]{3,1,2,0:T(8,128)(2,1)S(1)}, bf16[16,64,1,128]{3,1,2,0:T(8,128)(2,1)S(1)}, u32[]{:S(2)}, u32[]{:S(2)}) %collective-permute-start.8) | collective-permute-done | bytes 262176 | tf_op jit(solution)/shard_map/ppermute | solution.py:14
  117.2 8.5 %collective-permute-start.11 = (bf16[16,64,1,128]{3,1,2,0:T(8,128)(2,1)S(1)}, bf16[16,64,1,128]{3,1,2,0:T(8,128)(2,1)S(1)}, u32[]{:S(2)}, u32[]{:S(2)}) collective-permute-start(bf16[16,64,1,128]{3,1,2,0:T(8,128)(2,1)S(1)} %get-tuple-element.23), channel_id=1, source_target_pairs={{1,0},{2,1},{3,2},{4,3},{5,4},{6,5},{7,6},{0,7},{9,8},{10,9},{11,1... | collective-permute-start | bytes 786440 | tf_op jit(solution)/shard_map/ppermute | solution.py:17
  146.0 3.3 %collective-permute-start.12 = (bf16[16,64,1,128]{3,1,2,0:T(8,128)(2,1)S(1)}, bf16[16,64,1,128]{3,1,2,0:T(8,128)(2,1)}, u32[]{:S(2)}, u32[]{:S(2)}) collective-permute-start(bf16[16,64,1,128]{3,1,2,0:T(8,128)(2,1)S(1)} %fusion.26), channel_id=1, source_target_pairs={{0,1},{1,2},{2,3},{3,4},{4,5},{5,6},{6,7},{7,0},{8,9},{9,10},{10,1... | collective-permute-start | bytes 786440 | tf_op jit(solution)/shard_map/ppermute | solution.py:14
  161.1 2.4 convolution_bitcast_fusion.1
  163.9 4.6 %collective-permute-start.14 = (f32[32,1,2,576]{3,0,2,1:T(8,128)S(1)}, f32[32,1,2,576]{3,0,2,1:T(8,128)S(1)}, u32[]{:S(2)}, u32[]{:S(2)}) collective-permute-start(f32[32,1,2,576]{3,0,2,1:T(8,128)S(1)} %slice_select_fusion.1), channel_id=1, source_target_pairs={{0,16},{8,24},{16,0},{24,8},{32,48},{40,56},{48,32},{56,40},{64,80... | collective-permute-start | bytes 442376 | tf_op jit(solution)/shard_map/ppermute | solution.py:25
  168.6 2.6 fusion.20
  171.2 4.1 %collective-permute-start.16 = (f32[8,64,1,128]{3,1,2,0:T(8,128)S(1)}, f32[8,64,1,128]{3,1,2,0:T(8,128)S(1)}, u32[]{:S(2)}, u32[]{:S(2)}) collective-permute-start(f32[8,64,1,128]{3,1,2,0:T(8,128)S(1)} %slice_select_fusion), channel_id=1, source_target_pairs={{0,256},{8,264},{16,272},{24,280},{32,288},{40,296},{48,304},{56,3... | collective-permute-start | bytes 786440 | tf_op jit(solution)/shard_map/ppermute | solution.py:25
  175.6 12.3 %collective-permute-done.16 = f32[8,64,1,128]{3,1,2,0:T(8,128)S(1)} collective-permute-done((f32[8,64,1,128]{3,1,2,0:T(8,128)S(1)}, f32[8,64,1,128]{3,1,2,0:T(8,128)S(1)}, u32[]{:S(2)}, u32[]{:S(2)}) %collective-permute-start.16) | collective-permute-done | bytes 262176 | tf_op jit(solution)/shard_map/ppermute | solution.py:25
  188.0 7.0 %collective-permute-start.17 = (f32[4,64,1,128]{3,1,2,0:T(8,128)S(1)}, f32[4,64,1,128]{3,1,2,0:T(8,128)S(1)}, u32[]{:S(2)}, u32[]{:S(2)}) collective-permute-start(f32[4,64,1,128]{3,1,2,0:T(8,128)S(1)} %slice_select_fusion.2), channel_id=1, source_target_pairs={{0,128},{8,136},{16,144},{24,152},{32,160},{40,168},{48,176},{56,1... | collective-permute-start | bytes 393224 | tf_op jit(solution)/shard_map/ppermute | solution.py:25
  197.6 11.2 %collective-permute-start.18 = (f32[2,64,1,128]{3,1,2,0:T(8,128)S(1)}, f32[2,64,1,128]{3,1,2,0:T(8,128)S(1)}, u32[]{:S(2)}, u32[]{:S(2)}) collective-permute-start(f32[2,64,1,128]{3,1,2,0:T(8,128)S(1)} %slice_select_fusion.4), channel_id=1, source_target_pairs={{0,64},{8,72},{16,80},{24,88},{32,96},{40,104},{48,112},{56,120},{... | collective-permute-start | bytes 196616 | tf_op jit(solution)/shard_map/ppermute | solution.py:25
  210.5 5.8 %collective-permute-start.19 = (f32[1,64,1,128]{3,1,2,0:T(8,128)S(1)}, f32[1,64,1,128]{3,1,2,0:T(8,128)S(1)}, u32[]{:S(2)}, u32[]{:S(2)}) collective-permute-start(f32[1,64,1,128]{3,1,2,0:T(8,128)S(1)} %slice_select_fusion.5), channel_id=1, source_target_pairs={{0,32},{8,40},{16,48},{24,56},{32,0},{40,8},{48,16},{56,24},{64,96... | collective-permute-start | bytes 98312 | tf_op jit(solution)/shard_map/ppermute | solution.py:25
  216.3 16.9 %all-gather = f32[128,1,2,576]{3,2,1,0:T(2,128)S(1)} all-gather(f32[16,1,2,576]{3,2,1,0:T(2,128)S(1)} %copy.53), channel_id=2, replica_groups=mesh['state'=64,'lat'=8] {'lat'}, dimensions={0}, use_global_device_ids=true | all-gather | bytes 663552 | tf_op jit(solution)/shard_map/all_gather | solution.py:192
  235.6 95.9 %all-reduce = (f32[16,64]{1,0:T(8,128)}, f32[64,9]{0,1:T(8,128)}) all-reduce(f32[16,64]{1,0:T(8,128)S(1)} %broadcast_multiply_fusion.1, f32[64,9]{0,1:T(8,128)S(1)} %stack.47), channel_id=1, replica_groups=mesh['state'=64,'lat'=8] {'state','lat'}, use_global_device_ids=true, to_apply=%region_1.2 | all-reduce | flops 1600 | bytes 12800 | tf_op jit(solution)/shard_map/psum | solution.py:189
  (184 shorter events, 67.1 us)
Async XLA Ops:
  1.5 10.7 %collective-permute-start.1 = (bf16[1,1,1,128]{3,2,1,0:T(2,128)(2,1)S(1)}, bf16[1,1,1,128]{3,2,1,0:T(2,128)(2,1)S(1)}, u32[]{:S(2)}, u32[]{:S(2)}) collective-permute-start(bf16[1,1,1,128]{3,2,1,0:T(2,128)(2,1)S(1)} %convert_bitcast_fusion), channel_id=1, source_target_pairs={{1,0},{2,1},{3,2},{4,3},{5,4},{6,5},{7,6},{0,7},{9,8},{10,9},{11,1... | collective-permute-start | bytes 776 | tf_op jit(solution)/shard_map/ppermute | solution.py:17
  10.2 3.0 collective-permute-start
  18.8 7.5 %collective-permute-start.3 = (bf16[1,64,1,128]{3,1,2,0:T(8,128)(2,1)S(1)}, bf16[1,64,1,128]{3,1,2,0:T(8,128)(2,1)S(1)}, u32[]{:S(2)}, u32[]{:S(2)}) collective-permute-start(bf16[1,64,1,128]{3,1,2,0:T(8,128)(2,1)S(1)} %fusion.29), channel_id=1, source_target_pairs={{1,0},{2,1},{3,2},{4,3},{5,4},{6,5},{7,6},{0,7},{9,8},{10,9},{11,1... | collective-permute-start | bytes 49160 | tf_op jit(solution)/shard_map/ppermute | solution.py:17
  24.3 3.1 collective-permute-start.2
  27.6 5.4 %collective-permute-start.4 = (bf16[1,64,3,130]{3,1,2,0:T(8,128)(2,1)S(1)}, bf16[1,64,3,130]{3,1,2,0:T(8,128)(2,1)S(1)}, u32[]{:S(2)}, u32[]{:S(2)}) collective-permute-start(bf16[1,64,3,130]{3,1,2,0:T(8,128)(2,1)S(1)} %pad_maximum_fusion.21), channel_id=1, source_target_pairs={{0,32},{8,40},{16,48},{24,56},{32,0},{40,8},{48,16},{56,24},{64,96... | collective-permute-start | bytes 149768 | tf_op jit(solution)/shard_map/ppermute | solution.py:25
  33.1 9.5 %collective-permute-start.5 = (bf16[2,64,3,130]{3,1,2,0:T(8,128)(2,1)S(1)}, bf16[2,64,3,130]{3,1,2,0:T(8,128)(2,1)}, u32[]{:S(2)}, u32[]{:S(2)}) collective-permute-start(bf16[2,64,3,130]{3,1,2,0:T(8,128)(2,1)S(1)} %maximum_select_fusion.3), channel_id=1, source_target_pairs={{0,64},{8,72},{16,80},{24,88},{32,96},{40,104},{48,112},{56,120},{... | collective-permute-start | bytes 299528 | tf_op jit(solution)/shard_map/ppermute | solution.py:25
  43.8 15.8 %collective-permute-start.6 = (bf16[4,64,3,130]{3,1,2,0:T(8,128)(2,1)S(1)}, bf16[4,64,3,130]{3,1,2,0:T(8,128)(2,1)S(1)}, u32[]{:S(2)}, u32[]{:S(2)}) collective-permute-start(bf16[4,64,3,130]{3,1,2,0:T(8,128)(2,1)S(1)} %maximum_select_fusion.2), channel_id=1, source_target_pairs={{0,128},{8,136},{16,144},{24,152},{32,160},{40,168},{48,176},{56,1... | collective-permute-start | bytes 599048 | tf_op jit(solution)/shard_map/ppermute | solution.py:25
  59.9 17.6 %collective-permute-start.7 = (bf16[8,64,3,130]{3,1,2,0:T(8,128)(2,1)S(1)}, bf16[8,64,3,130]{3,1,2,0:T(8,128)(2,1)S(1)}, u32[]{:S(2)}, u32[]{:S(2)}) collective-permute-start(bf16[8,64,3,130]{3,1,2,0:T(8,128)(2,1)S(1)} %maximum_select_fusion.1), channel_id=1, source_target_pairs={{0,256},{8,264},{16,272},{24,280},{32,288},{40,296},{48,304},{56,3... | collective-permute-start | bytes 1198088 | tf_op jit(solution)/shard_map/ppermute | solution.py:25
  80.9 23.0 %collective-permute-start.9 = (bf16[16,64,1,128]{3,1,2,0:T(8,128)(2,1)S(1)}, bf16[16,64,1,128]{3,1,2,0:T(8,128)(2,1)S(1)}, u32[]{:S(2)}, u32[]{:S(2)}) collective-permute-start(bf16[16,64,1,128]{3,1,2,0:T(8,128)(2,1)S(1)} %get-tuple-element.37), channel_id=1, source_target_pairs={{1,0},{2,1},{3,2},{4,3},{5,4},{6,5},{7,6},{0,7},{9,8},{10,9},{11,1... | collective-permute-start | bytes 786440 | tf_op jit(solution)/shard_map/ppermute | solution.py:17
  91.2 22.0 %collective-permute-start.8 = (bf16[16,64,1,128]{3,1,2,0:T(8,128)(2,1)S(1)}, bf16[16,64,1,128]{3,1,2,0:T(8,128)(2,1)S(1)}, u32[]{:S(2)}, u32[]{:S(2)}) collective-permute-start(bf16[16,64,1,128]{3,1,2,0:T(8,128)(2,1)S(1)} %get-tuple-element.37), channel_id=1, source_target_pairs={{0,1},{1,2},{2,3},{3,4},{4,5},{5,6},{6,7},{7,0},{8,9},{9,10},{10,1... | collective-permute-start | bytes 786440 | tf_op jit(solution)/shard_map/ppermute | solution.py:14
  117.2 19.3 %collective-permute-start.11 = (bf16[16,64,1,128]{3,1,2,0:T(8,128)(2,1)S(1)}, bf16[16,64,1,128]{3,1,2,0:T(8,128)(2,1)S(1)}, u32[]{:S(2)}, u32[]{:S(2)}) collective-permute-start(bf16[16,64,1,128]{3,1,2,0:T(8,128)(2,1)S(1)} %get-tuple-element.23), channel_id=1, source_target_pairs={{1,0},{2,1},{3,2},{4,3},{5,4},{6,5},{7,6},{0,7},{9,8},{10,9},{11,1... | collective-permute-start | bytes 786440 | tf_op jit(solution)/shard_map/ppermute | solution.py:17
  125.6 10.9 %collective-permute-start.10 = (bf16[16,64,1,128]{3,1,2,0:T(8,128)(2,1)S(1)}, bf16[16,64,1,128]{3,1,2,0:T(8,128)(2,1)}, u32[]{:S(2)}, u32[]{:S(2)}) collective-permute-start(bf16[16,64,1,128]{3,1,2,0:T(8,128)(2,1)S(1)} %get-tuple-element.23), channel_id=1, source_target_pairs={{0,1},{1,2},{2,3},{3,4},{4,5},{5,6},{6,7},{7,0},{8,9},{9,10},{10,1... | collective-permute-start | bytes 786440 | tf_op jit(solution)/shard_map/ppermute | solution.py:14
  143.6 10.9 %collective-permute-start.13 = (bf16[16,64,1,128]{3,1,2,0:T(8,128)(2,1)S(1)}, bf16[16,64,1,128]{3,1,2,0:T(8,128)(2,1)S(1)}, u32[]{:S(2)}, u32[]{:S(2)}) collective-permute-start(bf16[16,64,1,128]{3,1,2,0:T(8,128)(2,1)S(1)} %fusion.26), channel_id=1, source_target_pairs={{1,0},{2,1},{3,2},{4,3},{5,4},{6,5},{7,6},{0,7},{9,8},{10,9},{11,1... | collective-permute-start | bytes 786440 | tf_op jit(solution)/shard_map/ppermute | solution.py:17
  146.0 9.2 %collective-permute-start.12 = (bf16[16,64,1,128]{3,1,2,0:T(8,128)(2,1)S(1)}, bf16[16,64,1,128]{3,1,2,0:T(8,128)(2,1)}, u32[]{:S(2)}, u32[]{:S(2)}) collective-permute-start(bf16[16,64,1,128]{3,1,2,0:T(8,128)(2,1)S(1)} %fusion.26), channel_id=1, source_target_pairs={{0,1},{1,2},{2,3},{3,4},{4,5},{5,6},{6,7},{7,0},{8,9},{9,10},{10,1... | collective-permute-start | bytes 786440 | tf_op jit(solution)/shard_map/ppermute | solution.py:14
  163.9 11.5 %collective-permute-start.14 = (f32[32,1,2,576]{3,0,2,1:T(8,128)S(1)}, f32[32,1,2,576]{3,0,2,1:T(8,128)S(1)}, u32[]{:S(2)}, u32[]{:S(2)}) collective-permute-start(f32[32,1,2,576]{3,0,2,1:T(8,128)S(1)} %slice_select_fusion.1), channel_id=1, source_target_pairs={{0,16},{8,24},{16,0},{24,8},{32,48},{40,56},{48,32},{56,40},{64,80... | collective-permute-start | bytes 442376 | tf_op jit(solution)/shard_map/ppermute | solution.py:25
  171.2 16.6 %collective-permute-start.16 = (f32[8,64,1,128]{3,1,2,0:T(8,128)S(1)}, f32[8,64,1,128]{3,1,2,0:T(8,128)S(1)}, u32[]{:S(2)}, u32[]{:S(2)}) collective-permute-start(f32[8,64,1,128]{3,1,2,0:T(8,128)S(1)} %slice_select_fusion), channel_id=1, source_target_pairs={{0,256},{8,264},{16,272},{24,280},{32,288},{40,296},{48,304},{56,3... | collective-permute-start | bytes 786440 | tf_op jit(solution)/shard_map/ppermute | solution.py:25
  175.6 59.3 %copy-start.16 = (bf16[1,1,1,128]{3,2,1,0:T(2,128)(2,1)S(1)}, bf16[1,1,1,128]{3,2,1,0:T(2,128)(2,1)}, u32[]{:S(2)}) copy-start(bf16[1,1,1,128]{3,2,1,0:T(2,128)(2,1)} %get-tuple-element.12) | copy-start | bytes 772
  175.6 59.5 %copy-start.11 = (bf16[1,1,1,128]{3,2,1,0:T(2,128)(2,1)S(1)}, bf16[1,1,1,128]{3,2,1,0:T(2,128)(2,1)}, u32[]{:S(2)}) copy-start(bf16[1,1,1,128]{3,2,1,0:T(2,128)(2,1)} %get-tuple-element.22) | copy-start | bytes 772
  175.6 59.6 %copy-start.7 = (bf16[1,1,1,128]{3,2,1,0:T(2,128)(2,1)S(1)}, bf16[1,1,1,128]{3,2,1,0:T(2,128)(2,1)}, u32[]{:S(2)}) copy-start(bf16[1,1,1,128]{3,2,1,0:T(2,128)(2,1)} %copy-done.6) | copy-start | bytes 772
  175.6 59.8 %copy-start.5 = (bf16[1,1,1,128]{3,2,1,0:T(2,128)(2,1)S(1)}, bf16[1,1,1,128]{3,2,1,0:T(2,128)(2,1)}, u32[]{:S(2)}) copy-start(bf16[1,1,1,128]{3,2,1,0:T(2,128)(2,1)} %copy-done.4) | copy-start | bytes 772
  188.0 9.6 %collective-permute-start.17 = (f32[4,64,1,128]{3,1,2,0:T(8,128)S(1)}, f32[4,64,1,128]{3,1,2,0:T(8,128)S(1)}, u32[]{:S(2)}, u32[]{:S(2)}) collective-permute-start(f32[4,64,1,128]{3,1,2,0:T(8,128)S(1)} %slice_select_fusion.2), channel_id=1, source_target_pairs={{0,128},{8,136},{16,144},{24,152},{32,160},{40,168},{48,176},{56,1... | collective-permute-start | bytes 393224 | tf_op jit(solution)/shard_map/ppermute | solution.py:25
  195.0 13.8 %collective-permute-start.15 = (f32[16,1,2,576]{3,0,2,1:T(8,128)S(1)}, f32[16,1,2,576]{3,0,2,1:T(8,128)S(1)}, u32[]{:S(2)}, u32[]{:S(2)}) collective-permute-start(f32[16,1,2,576]{3,0,2,1:T(8,128)S(1)} %slice_select_fusion.3), channel_id=1, source_target_pairs={{0,8},{8,0},{16,24},{24,16},{32,40},{40,32},{48,56},{56,48},{64,72... | collective-permute-start | bytes 221192 | tf_op jit(solution)/shard_map/ppermute | solution.py:25
  197.6 12.9 %collective-permute-start.18 = (f32[2,64,1,128]{3,1,2,0:T(8,128)S(1)}, f32[2,64,1,128]{3,1,2,0:T(8,128)S(1)}, u32[]{:S(2)}, u32[]{:S(2)}) collective-permute-start(f32[2,64,1,128]{3,1,2,0:T(8,128)S(1)} %slice_select_fusion.4), channel_id=1, source_target_pairs={{0,64},{8,72},{16,80},{24,88},{32,96},{40,104},{48,112},{56,120},{... | collective-permute-start | bytes 196616 | tf_op jit(solution)/shard_map/ppermute | solution.py:25
  210.5 23.6 %collective-permute-start.19 = (f32[1,64,1,128]{3,1,2,0:T(8,128)S(1)}, f32[1,64,1,128]{3,1,2,0:T(8,128)S(1)}, u32[]{:S(2)}, u32[]{:S(2)}) collective-permute-start(f32[1,64,1,128]{3,1,2,0:T(8,128)S(1)} %slice_select_fusion.5), channel_id=1, source_target_pairs={{0,32},{8,40},{16,48},{24,56},{32,0},{40,8},{48,16},{56,24},{64,96... | collective-permute-start | bytes 98312 | tf_op jit(solution)/shard_map/ppermute | solution.py:25
  (18 other events, 453.7 us)
